TPU v7x, 512 devices: a whole 4x8x8 slice. The times are simulated.
512 devices in a mesh: region: 32 (over x, y), shard: 16 (over z, core).
Axes of the slice: x: 4, y: 8, z: 8, core: 2. Of those that a mesh axis runs over, the one named last changes fastest.
Arguments:
- state_anom: float32 [524288, 256], P(('region', 'shard')), may hold values from -6 to 6
- state_mean: float32 [524288], P(('region', 'shard')), may hold values from -6 to 6
- obs_anom: float32 [64, 512, 256], P('region', 'shard'), may hold values from -6 to 6
- obs_depart: float32 [64, 512], P('region', 'shard'), may hold values from -6 to 6
- obs_var: float32 [64, 512], P('region', 'shard'), may hold values from 0.5 to 2
- taper_levels: float32 [8], replicated, may hold values from 0 to 1
- state_taper: int32 [4096, 256], P(('region', 'shard')), may hold values from 0 to 7
- obs_taper: int32 [256, 256], P('region'), may hold values from 0 to 7
- batch_order: int32 [3], replicated, may hold values from 0 to 63, as said below
Outputs:
- post_anom: float32 [524288, 256], P(('region', 'shard'))
- post_mean: float32 [524288], P(('region', 'shard'))
- post_obs_anom: float32 [64, 512, 256], P('region', 'shard')
- post_obs_depart: float32 [64, 512], P('region', 'shard')
Inputs may be any that keep to these rules, and one draw needn't show every extreme that they name: `batch_order`: 3 distinct batch numbers; batch q lies in region q // 2; the first and the last batch number both occur.
All inputs are finite; a program needn't handle non-finite values.
Results may differ from a plain program's by a relative error of at most 0.0001.
Values sent between devices are 32-bit elements; how exact they have to be, the bound alone decides.
No kernel may reach another device: no remote copies, remote signals or barrier semaphores. Data moves between devices by JAX's collectives and lax.ppermute only.
A program may use at most 64 MiB of HBM per device.

v0:
```python
import jax
import jax.numpy as jnp
from jax import lax
from jax.sharding import PartitionSpec as P

M = 256
P_SIZE = 512
TAPER_BLOCK = 128
NB = 3
KB = 2
highest = lax.Precision.HIGHEST


def from_root(block, axis, source):
    block = jnp.where(lax.axis_index(axis) == source, block, jnp.zeros_like(block))
    return lax.psum(block, axis)


def factorize(anomalies, departs, variances):
    product = jnp.dot(anomalies, anomalies.T, precision=highest, preferred_element_type=jnp.float32)
    system = product / (M - 1) + jnp.diag(variances)
    lower_factor = jnp.linalg.cholesky(system)
    shifted = lower_factor + jnp.diag(jnp.sqrt(variances))
    solved = lax.linalg.triangular_solve(shifted, anomalies, left_side=True, lower=True)
    increments = lax.linalg.triangular_solve(
        lower_factor, solved, left_side=True, lower=True, transpose_a=True
    )
    first = lax.linalg.triangular_solve(lower_factor, departs[:, None], left_side=True, lower=True)
    weights = lax.linalg.triangular_solve(
        lower_factor, first, left_side=True, lower=True, transpose_a=True
    )
    return (increments, weights[:, 0])


def lookup(levels, index):
    levels_count = levels.shape[0]
    onehot = (index[..., None] == jnp.arange(levels_count, dtype=jnp.int32)).astype(jnp.float32)
    return jnp.sum(onehot * levels, axis=-1)


def covariance(rows, batch_rows):
    product = lax.dot_general(
        rows,
        batch_rows,
        (((1,), (1,)), ((), ())),
        precision=highest,
        preferred_element_type=jnp.float32,
    )
    return product / (M - 1)


def apply_rows(covar, increments, weights):
    delta_rows = jnp.dot(covar, increments, precision=highest, preferred_element_type=jnp.float32)
    delta_mean = jnp.dot(covar, weights, precision=highest, preferred_element_type=jnp.float32)
    return (delta_rows, delta_mean)


def per_device(
    state_anom,
    state_mean,
    obs_anom,
    obs_depart,
    obs_var,
    taper_levels,
    state_taper,
    obs_taper,
    batch_order,
):
    shard_pos = lax.axis_index("shard")
    pieces = obs_anom.shape[1]
    blocks = P_SIZE // TAPER_BLOCK
    obs_rows = obs_anom.shape[0] * pieces
    state_rows = state_anom.shape[0]
    row_block = (
        jnp.arange(KB, dtype=jnp.int32)[:, None] * P_SIZE
        + shard_pos * pieces
        + jnp.arange(pieces, dtype=jnp.int32)[None, :]
    ).reshape(obs_rows) // TAPER_BLOCK
    anomaly = state_anom
    mean_state = state_mean
    obs_now = obs_anom.reshape(obs_rows, M)
    depart_now = obs_depart.reshape(obs_rows)
    for section_idx in range(NB):
        batch_id = batch_order[section_idx]
        owner_id = batch_id // KB
        local_id = batch_id % KB
        rows_piece = lax.dynamic_slice_in_dim(obs_now, local_id * pieces, pieces, 0)
        depart_piece = lax.dynamic_slice_in_dim(depart_now, local_id * pieces, pieces, 0)
        var_piece = lax.dynamic_index_in_dim(obs_var, local_id, 0, keepdims=False)
        sent_rows, sent_depart, sent_var = (
            from_root(rows_piece, "region", owner_id),
            from_root(depart_piece, "region", owner_id),
            from_root(var_piece, "region", owner_id),
        )
        batch_rows, departs, variances = (
            lax.all_gather(sent_rows, "shard", axis=0, tiled=True),
            lax.all_gather(sent_depart, "shard", axis=0, tiled=True),
            lax.all_gather(sent_var, "shard", axis=0, tiled=True),
        )
        increments, weights = factorize(batch_rows, departs, variances)
        state_cols = lax.dynamic_slice_in_dim(state_taper, batch_id * blocks, blocks, 1)
        state_weights = lookup(taper_levels, state_cols)
        covar = covariance(anomaly, batch_rows)
        covar = (
            covar.reshape(state_rows // TAPER_BLOCK, TAPER_BLOCK, blocks, TAPER_BLOCK)
            * state_weights[:, None, :, None]
        )
        covar = covar.reshape(state_rows, P_SIZE)
        delta_rows, delta_mean = apply_rows(covar, increments, weights)
        obs_cols = lax.dynamic_slice_in_dim(obs_taper, batch_id * blocks, blocks, 1)
        obs_weights = lookup(taper_levels, jnp.take(obs_cols, row_block, axis=0))
        covar_obs = (
            covariance(obs_now, batch_rows).reshape(obs_rows, blocks, TAPER_BLOCK)
            * obs_weights[:, :, None]
        )
        covar_obs = covar_obs.reshape(obs_rows, P_SIZE)
        delta_obs, delta_depart = apply_rows(covar_obs, increments, weights)
        anomaly = anomaly - delta_rows
        mean_state = mean_state + delta_mean
        obs_now = obs_now - delta_obs
        depart_now = depart_now - delta_depart
    return (
        anomaly,
        mean_state,
        obs_now.reshape(obs_anom.shape),
        depart_now.reshape(obs_depart.shape),
    )


def solution(mesh):
    placed = (
        P(("region", "shard"), None),
        P(("region", "shard")),
        P("region", "shard", None),
        P("region", "shard"),
        P("region", "shard"),
        P(),
        P(("region", "shard"), None),
        P("region", None),
        P(),
    )
    return jax.shard_map(
        per_device,
        mesh=mesh,
        in_specs=placed,
        out_specs=(
            P(("region", "shard"), None),
            P(("region", "shard")),
            P("region", "shard", None),
            P("region", "shard"),
        ),
        check_vma=False,
    )
```

profile of v0, /device:TPU:1, one launch (start us, length us, event | category | flops | bytes accessed | tf_op | source)
XLA Modules:
  0.0 1229.0 jit_solution(11346918617934155445)
XLA Ops:
  12.8 116.3 %all-reduce.9 = (f32[32,256]{1,0:T(8,128)S(1)}, f32[32]{0:T(128)S(1)}, f32[32]{0:T(128)S(1)}) all-reduce(f32[32,256]{1,0:T(8,128)S(1)} %dynamic-slice_select_fusion.2, f32[32]{0:T(128)S(1)} %get-tuple-element.312, f32[32]{0:T(128)S(1)} %broadcast_select_fusion.5), channel_id=1, replica_groups=mesh['region'=32,'shard'=16] {'region'}, use_global_device_ids=true, to_apply=%region_0.1 | all-reduce | flops 8256 | bytes 66048 | tf_op jit(solution)/shard_map/psum | solution.py:16
  131.5 57.6 %all-reduce.12 = (f32[512]{0:T(512)S(1)}, f32[512]{0:T(512)S(1)}) all-reduce(f32[512]{0:T(512)S(1)} %dynamic-update-slice.30, f32[512]{0:T(512)S(1)} %dynamic-update-slice.33), channel_id=1, replica_groups=mesh['region'=32,'shard'=16] {'shard'}, use_global_device_ids=true, to_apply=%add.1 | all-reduce | flops 1024 | bytes 8192
  189.1 15.9 %all_gather.27 = f32[512,256]{1,0:T(8,128)S(1)} all-gather(f32[32,256]{1,0:T(8,128)S(1)} %get-tuple-element.258), channel_id=1, replica_groups=mesh['region'=32,'shard'=16] {'shard'}, dimensions={0}, use_global_device_ids=true | all-gather | bytes 557056 | tf_op jit(solution)/shard_map/all_gather | solution.py:96
  207.6 11.7 cholesky.374
  231.7 11.7 cholesky.393
  257.7 11.7 cholesky.414
  282.4 12.1 cholesky.431
  305.7 39.3 %custom-call.50 = f32[4,128,128]{1,2,0:T(8,128)S(1)} custom-call(f32[4,128,128]{2,1,0:T(8,128)S(1)} %get-tuple-element.91), custom_call_target="InvertDiagBlocksLowerTriangular" | custom-call | tf_op jit(solution)/shard_map/triangular_solve/custom-call.8 | solution.py:25
  354.8 11.6 while.24
  366.5 39.3 %custom-call.49 = f32[4,128,128]{1,2,0:T(8,128)S(1)} custom-call(f32[4,128,128]{2,1,0:T(8,128)S(1)} %get-tuple-element.90), custom_call_target="InvertDiagBlocksLowerTriangular" | custom-call | tf_op jit(solution)/shard_map/triangular_solve/custom-call.3 | solution.py:24
  413.5 110.3 %all-reduce.8 = (f32[32,256]{1,0:T(8,128)S(1)}, f32[32]{0:T(128)S(1)}, f32[32]{0:T(128)S(1)}) all-reduce(f32[32,256]{1,0:T(8,128)S(1)} %dynamic-slice_select_fusion.1, f32[32]{0:T(128)S(1)} %copy-done.62, f32[32]{0:T(128)S(1)} %broadcast_select_fusion.4), channel_id=1, replica_groups=mesh['region'=32,'shard'=16] {'region'}, use_global_device_ids=true, to_apply=%region_12.17 | all-reduce | flops 8256 | bytes 66048 | tf_op jit(solution)/shard_map/psum | solution.py:16
  524.2 51.0 %all-reduce.11 = (f32[512]{0:T(512)S(1)}, f32[512]{0:T(512)}) all-reduce(f32[512]{0:T(512)S(1)} %dynamic-update-slice.31, f32[512]{0:T(512)S(1)} %dynamic-update-slice.34), channel_id=1, replica_groups=mesh['region'=32,'shard'=16] {'shard'}, use_global_device_ids=true, to_apply=%add.2 | all-reduce | flops 1024 | bytes 8192
  575.2 16.4 %all_gather.29 = f32[512,256]{1,0:T(8,128)S(1)} all-gather(f32[32,256]{1,0:T(8,128)S(1)} %get-tuple-element.255), channel_id=1, replica_groups=mesh['region'=32,'shard'=16] {'shard'}, dimensions={0}, use_global_device_ids=true | all-gather | bytes 557056 | tf_op jit(solution)/shard_map/all_gather | solution.py:96
  594.2 11.7 cholesky.446
  618.3 11.7 cholesky.465
  645.2 11.7 cholesky.486
  669.8 11.9 cholesky.503
  692.9 39.3 %custom-call.55 = f32[4,128,128]{1,2,0:T(8,128)S(1)} custom-call(f32[4,128,128]{2,1,0:T(8,128)S(1)} %get-tuple-element.93), custom_call_target="InvertDiagBlocksLowerTriangular" | custom-call | tf_op jit(solution)/shard_map/triangular_solve/custom-call.8 | solution.py:25
  737.0 12.5 %while.26 = (s32[]{:T(128)}, f32[512,512]{0,1:T(8,128)}, s32[4,2]{0,1:T(2,128)S(1)}, f32[4,128,128]{2,1,0:T(8,128)S(1)}, s32[]{:T(128)}) while((s32[]{:T(128)}, f32[512,512]{0,1:T(8,128)}, s32[4,2]{0,1:T(2,128)S(1)}, f32[4,128,128]{2,1,0:T(8,128)S(1)}, s32[]{:T(128)}) %tuple.196), condition=%wide.while_cond.clone, body=%wide.while_body.clone.sunk | while | flops 2 | bytes 393321 | solution.py:24
  750.2 40.1 %custom-call.54 = f32[4,128,128]{1,2,0:T(8,128)S(1)} custom-call(f32[4,128,128]{2,1,0:T(8,128)} %copy-done.24), custom_call_target="InvertDiagBlocksLowerTriangular" | custom-call | tf_op jit(solution)/shard_map/triangular_solve/custom-call.3 | solution.py:24
  801.3 110.3 %all-reduce.7 = (f32[32,256]{1,0:T(8,128)S(1)}, f32[32]{0:T(128)S(1)}, f32[32]{0:T(128)S(1)}) all-reduce(f32[32,256]{1,0:T(8,128)S(1)} %dynamic-slice_select_fusion, f32[32]{0:T(128)S(1)} %copy-done.61, f32[32]{0:T(128)S(1)} %copy-done.63), channel_id=1, replica_groups=mesh['region'=32,'shard'=16] {'region'}, use_global_device_ids=true, to_apply=%region_16.21 | all-reduce | flops 8256 | bytes 66048 | tf_op jit(solution)/shard_map/psum | solution.py:16
  911.6 44.7 %all_gather.31 = f32[512,256]{1,0:T(8,128)S(1)} all-gather(f32[32,256]{1,0:T(8,128)S(1)} %get-tuple-element.252), channel_id=1, replica_groups=mesh['region'=32,'shard'=16] {'shard'}, dimensions={0}, use_global_device_ids=true | all-gather | bytes 557056 | tf_op jit(solution)/shard_map/all_gather | solution.py:96
  958.3 24.0 %all-reduce.10 = (f32[512]{0:T(512)S(1)}, f32[512]{0:T(512)}) all-reduce(f32[512]{0:T(512)S(1)} %dynamic-update-slice.32, f32[512]{0:T(512)S(1)} %dynamic-update-slice.35), channel_id=1, replica_groups=mesh['region'=32,'shard'=16] {'shard'}, use_global_device_ids=true, to_apply=%add.3 | all-reduce | flops 1024 | bytes 8192
  987.1 11.7 cholesky.518
  1011.2 11.7 cholesky.537
  1028.2 10.6 custom-call.57
  1040.7 11.7 cholesky.558
  1065.3 11.9 cholesky.575
  1080.3 12.5 %while.29 = (s32[]{:T(128)}, f32[512,512]{0,1:T(8,128)}, s32[4,2]{0,1:T(2,128)S(1)}, f32[4,128,128]{2,1,0:T(8,128)S(1)}, s32[]{:T(128)}) while((s32[]{:T(128)}, f32[512,512]{0,1:T(8,128)}, s32[4,2]{0,1:T(2,128)S(1)}, f32[4,128,128]{2,1,0:T(8,128)S(1)}, s32[]{:T(128)}) %tuple.197), condition=%wide.while_cond.1.clone.1, body=%wide.while_body.1.clone.1.sunk | while | flops 2 | bytes 393321 | solution.py:25
  1092.8 39.3 %custom-call.60 = f32[4,128,128]{1,2,0:T(8,128)S(1)} custom-call(f32[4,128,128]{2,1,0:T(8,128)S(1)} %get-tuple-element.95), custom_call_target="InvertDiagBlocksLowerTriangular" | custom-call | tf_op jit(solution)/shard_map/triangular_solve/custom-call.8 | solution.py:25
  1141.3 11.9 while.28
  1153.3 39.7 %custom-call.59 = f32[4,128,128]{1,2,0:T(8,128)S(1)} custom-call(f32[4,128,128]{2,1,0:T(8,128)S(1)} %get-tuple-element.94), custom_call_target="InvertDiagBlocksLowerTriangular" | custom-call | tf_op jit(solution)/shard_map/triangular_solve/custom-call.3 | solution.py:24
  (518 shorter events, 288.4 us)
Async XLA Ops:
  297.2 52.8 %copy-start.31 = (s32[8,256]{1,0:T(8,128)S(1)}, s32[8,256]{1,0:T(8,128)}, u32[]{:S(2)}) copy-start(s32[8,256]{1,0:T(8,128)} %param.27) | copy-start | bytes 24580
  297.2 52.8 %copy-start.32 = (s32[8,256]{1,0:T(8,128)S(1)}, s32[8,256]{1,0:T(8,128)}, u32[]{:S(2)}) copy-start(s32[8,256]{1,0:T(8,128)} %param.26) | copy-start | bytes 24580
  297.2 55.7 %copy-start.64 = (f32[8]{0:T(128)S(1)}, f32[8]{0:T(128)}, u32[]{:S(2)}) copy-start(f32[8]{0:T(128)} %param.25) | copy-start | bytes 100
  297.2 56.6 %copy-start.25 = (f32[2,32,256]{2,1,0:T(8,128)S(1)}, f32[2,32,256]{2,1,0:T(8,128)}, u32[]{:S(2)}) copy-start(f32[2,32,256]{2,1,0:T(8,128)} %param.22) | copy-start | bytes 196612
  346.9 7.9 copy-start.34
  347.4 7.5 copy-start.40
  347.9 6.9 copy-start.48
  354.7 54.6 %copy-start.56 = (f32[64]{0:T(128)}, f32[64]{0:T(128)S(1)}, u32[]{:S(2)}) copy-start(f32[64]{0:T(128)S(1)} %fusion.19) | copy-start | bytes 772
  412.3 179.2 %copy-start.9 = (f32[128,256]{1,0:T(8,128)}, f32[128,256]{1,0:T(8,128)S(1)}, u32[]{:S(2)}) copy-start(f32[128,256]{1,0:T(8,128)S(1)} %fusion.171) | copy-start | bytes 393220
  413.0 179.9 %copy-start.15 = (f32[128,256]{1,0:T(8,128)}, f32[128,256]{1,0:T(8,128)S(1)}, u32[]{:S(2)}) copy-start(f32[128,256]{1,0:T(8,128)S(1)} %fusion.170) | copy-start | bytes 393220
  413.4 161.8 %copy-start.26 = (f32[64,256]{1,0:T(8,128)}, f32[64,256]{1,0:T(8,128)S(1)}, u32[]{:S(2)}) copy-start(f32[64,256]{1,0:T(8,128)S(1)} %convolution_subtract_fusion.29) | copy-start | bytes 196612
  683.2 49.1 %copy-start.59 = (f32[512]{0:T(512)S(1)}, f32[512]{0:T(512)}, u32[]{:S(2)}) copy-start(f32[512]{0:T(512)} %get-tuple-element.264) | copy-start | bytes 6148
  684.4 50.7 %copy-start.46 = (f32[64,4]{0,1:T(4,128)S(1)}, f32[64,4]{0,1:T(4,128)}, u32[]{:S(2)}) copy-start(f32[64,4]{0,1:T(4,128)} %get-tuple-element.199) | copy-start | bytes 3076
  684.4 51.0 %copy-start.27 = (f32[64,256]{1,0:T(8,128)S(1)}, f32[64,256]{1,0:T(8,128)}, u32[]{:S(2)}) copy-start(f32[64,256]{1,0:T(8,128)} %copy-done.26) | copy-start | bytes 196612
  684.4 51.6 %copy-start.57 = (f32[64]{0:T(128)S(1)}, f32[64]{0:T(128)}, u32[]{:S(2)}) copy-start(f32[64]{0:T(128)} %copy-done.56) | copy-start | bytes 772
  734.2 57.2 %copy-start.36 = (f32[128,1]{0,1:T(1,128)}, f32[128,1]{0,1:T(1,128)S(1)}, u32[]{:S(2)}) copy-start(f32[128,1]{0,1:T(1,128)S(1)} %convolution_bitcast_fusion.18) | copy-start | bytes 1540
  734.6 56.7 %copy-start.42 = (f32[128,1]{0,1:T(1,128)}, f32[128,1]{0,1:T(1,128)S(1)}, u32[]{:S(2)}) copy-start(f32[128,1]{0,1:T(1,128)S(1)} %convolution_bitcast_fusion.16) | copy-start | bytes 1540
  735.2 57.3 %copy-start.50 = (f32[128,1]{0,1:T(1,128)}, f32[128,1]{0,1:T(1,128)S(1)}, u32[]{:S(2)}) copy-start(f32[128,1]{0,1:T(1,128)S(1)} %convolution_bitcast_fusion.15) | copy-start | bytes 1540
  736.3 59.9 %copy-start.54 = (f32[64]{0:T(128)}, f32[64]{0:T(128)S(1)}, u32[]{:S(2)}) copy-start(f32[64]{0:T(128)S(1)} %fusion.20) | copy-start | bytes 772
  796.1 4.7 copy-start.28
  799.6 112.0 %copy-start.5 = (f32[128,256]{1,0:T(8,128)}, f32[128,256]{1,0:T(8,128)S(1)}, u32[]{:S(2)}) copy-start(f32[128,256]{1,0:T(8,128)S(1)} %fusion.176) | copy-start | bytes 393220
  800.2 182.1 %copy-start.11 = (f32[128,256]{1,0:T(8,128)}, f32[128,256]{1,0:T(8,128)S(1)}, u32[]{:S(2)}) copy-start(f32[128,256]{1,0:T(8,128)S(1)} %fusion.175) | copy-start | bytes 393220
  800.9 110.8 %copy-start.17 = (f32[128,256]{1,0:T(8,128)}, f32[128,256]{1,0:T(8,128)S(1)}, u32[]{:S(2)}) copy-start(f32[128,256]{1,0:T(8,128)S(1)} %fusion.174) | copy-start | bytes 393220
  801.2 181.0 %copy-start.29 = (f32[64,256]{1,0:T(8,128)}, f32[64,256]{1,0:T(8,128)S(1)}, u32[]{:S(2)}) copy-start(f32[64,256]{1,0:T(8,128)S(1)} %convolution_subtract_fusion.28) | copy-start | bytes 196612
  1078.7 53.4 %copy-start.60 = (f32[512]{0:T(512)S(1)}, f32[512]{0:T(512)}, u32[]{:S(2)}) copy-start(f32[512]{0:T(512)} %get-tuple-element.262) | copy-start | bytes 6148
  1080.3 60.1 %copy-start.21 = (f32[64,512]{1,0:T(8,128)S(1)}, f32[64,512]{1,0:T(8,128)}, u32[]{:S(2)}) copy-start(f32[64,512]{1,0:T(8,128)} %fusion.3) | copy-start | bytes 393220
  1080.3 60.1 %copy-start.55 = (f32[64]{0:T(128)S(1)}, f32[64]{0:T(128)}, u32[]{:S(2)}) copy-start(f32[64]{0:T(128)} %copy-done.54) | copy-start | bytes 772
  1196.4 6.7 copy-start.22
  1196.4 6.7 copy-start.30
  1198.2 7.5 copy-start.33
  1201.4 6.0 copy-start
  1203.1 4.2 copy-start.19
  (33 other events, 65.3 us)
where the time goes:
time: 1240 us; the launch traced here: 1230 us
  blocking collectives  547 us (44%)
  other arithmetic  488 us (39%)
  local copies, waits for them, and re-layouts  86.3 us (7%)
  matrix products  86 us (7%)
  between operations  21.1 us (2%)
    psum x3, blocking collectives, from_root(): return lax.psum(block, axis)  337 us
    another operation x44, other arithmetic, factorize(): lower_factor = jnp.linalg.cholesky(system)  239 us
    unnamed x3, blocking collectives  133 us
    another operation x7, other arithmetic, factorize(): lax.linalg.triangular_solve(lower_factor, solved, left_side=True, lower=T...  122 us
    another operation x3, other arithmetic, factorize(): lax.linalg.triangular_solve(shifted, anomalies, left_side=True, lower=True)  119 us
    all_gather x3, blocking collectives, per_device(): lax.all_gather(sent_rows, 'shard', axis=0, tiled=True)  77 us
    another operation x60, local copies, waits for them, and re-layouts, factorize(): lax.linalg.triangular_solve(shifted, anomalies, left_side=True, lower=True)  35.6 us
    another operation x67, local copies, waits for them, and re-layouts, factorize(): lax.linalg.triangular_solve(lower_factor, solved, left_side=True, lower=T...  29 us

commit v1 on v0

--- a/solution.py
+++ b/solution.py
@@ -11,9 +11,15 @@
 highest = lax.Precision.HIGHEST
 
 
+def gather_and_add(x, axis):
+    shards = lax.all_gather(x, axis, axis=0, tiled=False)
+    total = shards.sum(axis=0)
+    return total
+
+
 def from_root(block, axis, source):
     block = jnp.where(lax.axis_index(axis) == source, block, jnp.zeros_like(block))
-    return lax.psum(block, axis)
+    return gather_and_add(block, axis)
 
 
 def factorize(anomalies, departs, variances):

time: 1240 us -> 1140 us (0.919)
  blocking collectives: 547 us -> 444 us
  between operations: 21.1 us -> 34.4 us
    psum x3 -> x0, blocking collectives: 337 us -> none  [from_root(): return lax.psum(block, axis)]
    unnamed x3 -> x6, blocking collectives: 133 us -> 303 us
    all_gather x0 -> x3, blocking collectives: none -> 76.5 us  [gather_and_add(): shards = lax.all_gather(x, axis, axis=0, tiled=False)]
    all_gather x3, blocking collectives: 77 us -> 64.4 us  [per_device(): lax.all_gather(sent_rows, 'shard', axis=0, tiled=True)]
  transfers between devices with their start and end apart: 0 -> 3, of which waited for: 0 -> 0; matrix products, arithmetic and copies ran while one was open for 0% -> 3% of each run, Pallas kernels for 0% -> 0%
where the time goes in v1:
time: 1140 us
  other arithmetic  491 us (43%)
  blocking collectives  444 us (39%)
  local copies, waits for them, and re-layouts  86.3 us (8%)
  matrix products  78.4 us (7%)
  between operations  34.4 us (3%)
    unnamed x6, blocking collectives  303 us
    another operation x44, other arithmetic, factorize(): lower_factor = jnp.linalg.cholesky(system)  238 us
    another operation x7, other arithmetic, factorize(): lax.linalg.triangular_solve(lower_factor, solved, left_side=True, lower=T...  123 us
    another operation x3, other arithmetic, factorize(): lax.linalg.triangular_solve(shifted, anomalies, left_side=True, lower=True)  118 us
    all_gather x3, blocking collectives, gather_and_add(): shards = lax.all_gather(x, axis, axis=0, tiled=False)  76.5 us
    all_gather x3, blocking collectives, per_device(): lax.all_gather(sent_rows, 'shard', axis=0, tiled=True)  64.4 us
    another operation x60, local copies, waits for them, and re-layouts, factorize(): lax.linalg.triangular_solve(shifted, anomalies, left_side=True, lower=True)  35.2 us
    another operation x67, local copies, waits for them, and re-layouts, factorize(): lax.linalg.triangular_solve(lower_factor, solved, left_side=True, lower=T...  25.5 us
  transfers between devices with their start and end apart: 3, of which 0 were waited for; matrix products, arithmetic and copies ran while one was open for 3% of the time, Pallas kernels for 0%

profile of v1, /device:TPU:1, one launch (start us, length us, event | category | flops | bytes accessed | tf_op | source)
XLA Modules:
  0.0 1135.6 jit_solution(17504180350228777656)
XLA Ops:
  25.0 62.1 %all-reduce.4 = f32[1024]{0:T(1024)S(1)} all-reduce(f32[1024]{0:T(1024)S(1)} %fusion.233), channel_id=5, replica_groups=mesh['region'=32,'shard'=16] {'region'}, use_global_device_ids=true, to_apply=%add.4 | all-reduce | flops 1024 | bytes 8192
  88.0 25.3 %all-gather.6 = f32[32,1,32]{2,1,0:T(1,128)S(1)} all-gather(f32[1,1,32]{2,1,0:T(1,128)S(1)} %get-tuple-element.351), channel_id=1, replica_groups=mesh['region'=32,'shard'=16] {'region'}, dimensions={0}, use_global_device_ids=true | all-gather | bytes 4224 | tf_op jit(solution)/shard_map/all_gather | solution.py:15
  113.9 51.5 %all-reduce.12 = (f32[512]{0:T(512)S(1)}, f32[512]{0:T(512)S(1)}) all-reduce(f32[512]{0:T(512)S(1)} %dynamic-update-slice.30, f32[512]{0:T(512)S(1)} %dynamic-update-slice.34), channel_id=1, replica_groups=mesh['region'=32,'shard'=16] {'shard'}, use_global_device_ids=true, to_apply=%add.1 | all-reduce | flops 1024 | bytes 8192
  173.1 25.4 %all-gather.7 = f32[32,1,32]{2,1,0:T(1,128)S(1)} all-gather(f32[1,1,32]{2,1,0:T(1,128)S(1)} %get-tuple-element.352), channel_id=1, replica_groups=mesh['region'=32,'shard'=16] {'region'}, dimensions={0}, use_global_device_ids=true | all-gather | bytes 4224 | tf_op jit(solution)/shard_map/all_gather | solution.py:15
  198.9 25.8 %all-gather.8 = f32[32,1,32]{2,1,0:T(1,128)S(1)} all-gather(f32[1,1,32]{2,1,0:T(1,128)S(1)} %get-tuple-element.350), channel_id=1, replica_groups=mesh['region'=32,'shard'=16] {'region'}, dimensions={0}, use_global_device_ids=true | all-gather | bytes 4224 | tf_op jit(solution)/shard_map/all_gather | solution.py:15
  226.3 31.8 %all_gather.77 = f32[512,256]{1,0:T(8,128)S(1)} all-gather(f32[32,256]{1,0:T(8,128)S(1)} %reduce_sum.135), channel_id=1, replica_groups=mesh['region'=32,'shard'=16] {'shard'}, dimensions={0}, use_global_device_ids=true | all-gather | bytes 557056 | tf_op jit(solution)/shard_map/all_gather | solution.py:102
  260.7 11.7 %cholesky.374 = f32[128,128]{1,0:T(8,128)S(1)} custom-call(f32[128,128]{1,0:T(8,128)S(1)} %cholesky.586), custom_call_target="Cholesky" | custom-call | tf_op jit(solution)/shard_map/jit(cholesky)/cholesky | solution.py:28
  284.8 11.7 %cholesky.393 = f32[128,128]{1,0:T(8,128)S(1)} custom-call(f32[128,128]{1,0:T(8,128)S(1)} %cholesky.590), custom_call_target="Cholesky" | custom-call | tf_op jit(solution)/shard_map/jit(cholesky)/cholesky | solution.py:28
  308.8 11.7 %cholesky.414 = f32[128,128]{1,0:T(8,128)S(1)} custom-call(f32[128,128]{1,0:T(8,128)S(1)} %cholesky.595), custom_call_target="Cholesky" | custom-call | tf_op jit(solution)/shard_map/jit(cholesky)/cholesky | solution.py:28
  332.1 11.9 %cholesky.431 = f32[128,128]{1,0:T(8,128)S(1)} custom-call(f32[128,128]{1,0:T(8,128)S(1)} %convolution_subtract_fusion.32), custom_call_target="Cholesky" | custom-call | tf_op jit(solution)/shard_map/jit(cholesky)/cholesky | solution.py:28
  349.9 11.7 %while.24 = (s32[]{:T(128)}, f32[512,512]{0,1:T(8,128)}, s32[4,2]{0,1:T(2,128)S(1)}, f32[4,128,128]{2,1,0:T(8,128)S(1)}, s32[]{:T(128)}) while((s32[]{:T(128)}, f32[512,512]{0,1:T(8,128)}, s32[4,2]{0,1:T(2,128)S(1)}, f32[4,128,128]{2,1,0:T(8,128)S(1)}, s32[]{:T(128)}) %tuple.188), condition=%wide.while_cond, body=%wide.while_body.sunk | while | flops 2 | bytes 393321 | solution.py:30
  361.7 39.3 %custom-call.49 = f32[4,128,128]{1,2,0:T(8,128)S(1)} custom-call(f32[4,128,128]{2,1,0:T(8,128)S(1)} %get-tuple-element.90), custom_call_target="InvertDiagBlocksLowerTriangular" | custom-call | tf_op jit(solution)/shard_map/triangular_solve/custom-call.3 | solution.py:30
  414.6 39.3 %custom-call.50 = f32[4,128,128]{1,2,0:T(8,128)S(1)} custom-call(f32[4,128,128]{2,1,0:T(8,128)S(1)} %get-tuple-element.91), custom_call_target="InvertDiagBlocksLowerTriangular" | custom-call | tf_op jit(solution)/shard_map/triangular_solve/custom-call.8 | solution.py:31
  463.4 58.6 %all-reduce.6 = f32[1024]{0:T(1024)S(1)} all-reduce(f32[1024]{0:T(1024)S(1)} %fusion.234), channel_id=6, replica_groups=mesh['region'=32,'shard'=16] {'region'}, use_global_device_ids=true, to_apply=%add.6 | all-reduce | flops 1024 | bytes 8192
  522.3 37.4 %all-reduce.11 = (f32[512]{0:T(512)S(1)}, f32[512]{0:T(512)}) all-reduce(f32[512]{0:T(512)} %copy-done.24, f32[512]{0:T(512)S(1)} %dynamic-update-slice.36), channel_id=1, replica_groups=mesh['region'=32,'shard'=16] {'shard'}, use_global_device_ids=true, to_apply=%add.2 | all-reduce | flops 1024 | bytes 8192
  569.0 16.4 %all_gather.82 = f32[512,256]{1,0:T(8,128)S(1)} all-gather(f32[32,256]{1,0:T(8,128)S(1)} %reduce_sum.139), channel_id=1, replica_groups=mesh['region'=32,'shard'=16] {'shard'}, dimensions={0}, use_global_device_ids=true | all-gather | bytes 557056 | tf_op jit(solution)/shard_map/all_gather | solution.py:102
  590.2 11.7 %cholesky.446 = f32[128,128]{1,0:T(8,128)S(1)} custom-call(f32[128,128]{1,0:T(8,128)S(1)} %cholesky.599), custom_call_target="Cholesky" | custom-call | tf_op jit(solution)/shard_map/jit(cholesky)/cholesky | solution.py:28
  614.3 11.7 %cholesky.465 = f32[128,128]{1,0:T(8,128)S(1)} custom-call(f32[128,128]{1,0:T(8,128)S(1)} %cholesky.603), custom_call_target="Cholesky" | custom-call | tf_op jit(solution)/shard_map/jit(cholesky)/cholesky | solution.py:28
  638.6 11.7 %cholesky.486 = f32[128,128]{1,0:T(8,128)S(1)} custom-call(f32[128,128]{1,0:T(8,128)S(1)} %cholesky.608), custom_call_target="Cholesky" | custom-call | tf_op jit(solution)/shard_map/jit(cholesky)/cholesky | solution.py:28
  662.0 11.9 %cholesky.503 = f32[128,128]{1,0:T(8,128)S(1)} custom-call(f32[128,128]{1,0:T(8,128)S(1)} %convolution_subtract_fusion.31), custom_call_target="Cholesky" | custom-call | tf_op jit(solution)/shard_map/jit(cholesky)/cholesky | solution.py:28
  682.3 11.9 %while.26 = (s32[]{:T(128)}, f32[512,512]{0,1:T(8,128)}, s32[4,2]{0,1:T(2,128)S(1)}, f32[4,128,128]{2,1,0:T(8,128)S(1)}, s32[]{:T(128)}) while((s32[]{:T(128)}, f32[512,512]{0,1:T(8,128)}, s32[4,2]{0,1:T(2,128)S(1)}, f32[4,128,128]{2,1,0:T(8,128)S(1)}, s32[]{:T(128)}) %tuple.214), condition=%wide.while_cond.clone, body=%wide.while_body.clone.sunk | while | flops 2 | bytes 393321 | solution.py:30
  694.2 39.3 %custom-call.54 = f32[4,128,128]{1,2,0:T(8,128)S(1)} custom-call(f32[4,128,128]{2,1,0:T(8,128)S(1)} %get-tuple-element.92), custom_call_target="InvertDiagBlocksLowerTriangular" | custom-call | tf_op jit(solution)/shard_map/triangular_solve/custom-call.3 | solution.py:30
  748.2 40.1 %custom-call.55 = f32[4,128,128]{1,2,0:T(8,128)S(1)} custom-call(f32[4,128,128]{2,1,0:T(8,128)} %copy-done.7), custom_call_target="InvertDiagBlocksLowerTriangular" | custom-call | tf_op jit(solution)/shard_map/triangular_solve/custom-call.8 | solution.py:31
  797.6 55.9 %all-reduce.8 = f32[1024]{0:T(1024)S(1)} all-reduce(f32[1024]{0:T(1024)S(1)} %fusion.235), channel_id=7, replica_groups=mesh['region'=32,'shard'=16] {'region'}, use_global_device_ids=true, to_apply=%add.8 | all-reduce | flops 1024 | bytes 8192
  853.8 37.2 %all-reduce.10 = (f32[512]{0:T(512)S(1)}, f32[512]{0:T(512)S(1)}) all-reduce(f32[512]{0:T(512)} %copy-done.25, f32[512]{0:T(512)S(1)} %dynamic-update-slice.38), channel_id=1, replica_groups=mesh['region'=32,'shard'=16] {'shard'}, use_global_device_ids=true, to_apply=%add.3 | all-reduce | flops 1024 | bytes 8192
  900.0 16.2 %all_gather.87 = f32[512,256]{1,0:T(8,128)S(1)} all-gather(f32[32,256]{1,0:T(8,128)S(1)} %reduce_sum.143), channel_id=1, replica_groups=mesh['region'=32,'shard'=16] {'shard'}, dimensions={0}, use_global_device_ids=true | all-gather | bytes 557056 | tf_op jit(solution)/shard_map/all_gather | solution.py:102
  918.9 11.7 %cholesky.518 = f32[128,128]{1,0:T(8,128)S(1)} custom-call(f32[128,128]{1,0:T(8,128)S(1)} %cholesky.612), custom_call_target="Cholesky" | custom-call | tf_op jit(solution)/shard_map/jit(cholesky)/cholesky | solution.py:28
  943.0 11.7 %cholesky.537 = f32[128,128]{1,0:T(8,128)S(1)} custom-call(f32[128,128]{1,0:T(8,128)S(1)} %cholesky.616), custom_call_target="Cholesky" | custom-call | tf_op jit(solution)/shard_map/jit(cholesky)/cholesky | solution.py:28
  990.4 11.9 %cholesky.575 = f32[128,128]{1,0:T(8,128)S(1)} custom-call(f32[128,128]{1,0:T(8,128)S(1)} %convolution_subtract_fusion.30), custom_call_target="Cholesky" | custom-call | tf_op jit(solution)/shard_map/jit(cholesky)/cholesky | solution.py:28
  1018.2 39.3 %custom-call.60 = f32[4,128,128]{1,2,0:T(8,128)S(1)} custom-call(f32[4,128,128]{2,1,0:T(8,128)S(1)} %get-tuple-element.95), custom_call_target="InvertDiagBlocksLowerTriangular" | custom-call | tf_op jit(solution)/shard_map/triangular_solve/custom-call.8 | solution.py:31
  1060.5 12.0 %while.28 = (s32[]{:T(128)}, f32[512,512]{0,1:T(8,128)}, s32[4,2]{0,1:T(2,128)S(1)}, f32[4,128,128]{2,1,0:T(8,128)S(1)}, s32[]{:T(128)}) while((s32[]{:T(128)}, f32[512,512]{0,1:T(8,128)}, s32[4,2]{0,1:T(2,128)S(1)}, f32[4,128,128]{2,1,0:T(8,128)S(1)}, s32[]{:T(128)}) %tuple.217), condition=%wide.while_cond.clone.1, body=%wide.while_body.clone.1.sunk | while | flops 2 | bytes 393321 | solution.py:30
  1072.5 39.6 %custom-call.59 = f32[4,128,128]{1,2,0:T(8,128)S(1)} custom-call(f32[4,128,128]{2,1,0:T(8,128)S(1)} %get-tuple-element.94), custom_call_target="InvertDiagBlocksLowerTriangular" | custom-call | tf_op jit(solution)/shard_map/triangular_solve/custom-call.3 | solution.py:30
  (480 shorter events, 316.2 us)
Async XLA Ops:
  7.2 217.8 %all-gather.13.cloned.1.call-start = ((), (), s32[]{:S(2)}) async-start(), calls=%async_computation | async-start | bytes 1081344 | tf_op jit(solution)/shard_map/all_gather | solution.py:15
  12.6 555.1 %all-gather.15.cloned.1.call-start = ((), (), s32[]{:S(2)}) async-start(), calls=%async_computation.1 | async-start | bytes 1081344 | tf_op jit(solution)/shard_map/all_gather | solution.py:15
  198.9 60.5 %copy-start.24 = (f32[512]{0:T(512)}, f32[512]{0:T(512)S(1)}, u32[]{:S(2)}) copy-start(f32[512]{0:T(512)S(1)} %dynamic-update-slice.31) | copy-start | bytes 6148
  224.9 34.5 %copy-start.25 = (f32[512]{0:T(512)}, f32[512]{0:T(512)S(1)}, u32[]{:S(2)}) copy-start(f32[512]{0:T(512)S(1)} %dynamic-update-slice.32) | copy-start | bytes 6148
  259.7 1.0 copy-start.3
  414.6 41.5 %copy-start.8 = (f32[2,32,256]{2,1,0:T(8,128)S(1)}, f32[2,32,256]{2,1,0:T(8,128)}, u32[]{:S(2)}) copy-start(f32[2,32,256]{2,1,0:T(8,128)} %param.22) | copy-start | bytes 196612
  457.2 0.6 copy-start.11
  457.8 102.8 %copy-start.2 = (f32[1024,256]{1,0:T(8,128)S(1)}, f32[1024,256]{1,0:T(8,128)}, u32[]{:S(2)}) copy-start(f32[1024,256]{1,0:T(8,128)} %param.20) | copy-start | bytes 3145732
  458.4 440.3 %all-gather.17.cloned.1.call-start = ((), (), s32[]{:S(2)}) async-start(), calls=%async_computation.2 | async-start | bytes 1081344 | tf_op jit(solution)/shard_map/all_gather | solution.py:15
  460.8 1.9 copy-start.18
  461.3 1.5 copy-start.22
  560.6 2.3 copy-start.19
  560.6 2.3 copy-start.23
  589.2 1.0 copy-start.4
  626.7 47.3 %copy-start.15 = (f32[64,4]{1,0:T(8,128)S(1)}, f32[64,4]{1,0:T(8,128)}, u32[]{:S(2)}) copy-start(f32[64,4]{1,0:T(8,128)} %copy.119) | copy-start | bytes 3076
  626.7 47.4 %copy-start.12 = (f32[64,256]{1,0:T(8,128)S(1)}, f32[64,256]{1,0:T(8,128)}, u32[]{:S(2)}) copy-start(f32[64,256]{1,0:T(8,128)} %copy-done.11) | copy-start | bytes 196612
  694.2 44.5 %copy-start.1 = (f32[512,512]{0,1:T(8,128)S(1)}, f32[512,512]{0,1:T(8,128)}, u32[]{:S(2)}) copy-start(f32[512,512]{0,1:T(8,128)} %get-tuple-element.584) | copy-start | bytes 3145732
  747.5 0.7 copy-start.7
  788.4 2.1 copy-start.13
  788.4 4.6 copy-start.30
  789.5 6.5 copy-start.6
  791.7 0.6 copy-start.9
  794.9 1.9 copy-start.16
  795.4 1.4 copy-start.20
  892.0 2.0 copy-start.17
  892.1 2.0 copy-start.21
  917.9 1.0 copy-start.5
  955.1 47.3 %copy-start.14 = (f32[64,4]{1,0:T(8,128)S(1)}, f32[64,4]{1,0:T(8,128)}, u32[]{:S(2)}) copy-start(f32[64,4]{1,0:T(8,128)} %copy.140) | copy-start | bytes 3076
  955.2 47.4 %copy-start.10 = (f32[64,256]{1,0:T(8,128)S(1)}, f32[64,256]{1,0:T(8,128)}, u32[]{:S(2)}) copy-start(f32[64,256]{1,0:T(8,128)} %copy-done.9) | copy-start | bytes 196612
  1115.5 3.8 copy-start.28
  1118.6 2.3 copy-start
  1124.8 3.5 copy-start.29
  (3 other events, 1.8 us)
Sparse Core Ops, SparseCore 0:
  12.7 82.1 all-gather.12
  458.6 70.8 all-gather.14
  793.1 67.7 all-gather.16
